TPU v7x, 32 devices: a whole 2x2x4 slice. The times are simulated.
32 devices in a mesh: groups: 2 (over y), coord: 8 (over z, x), ckpt: 2 (over core).
Axes of the slice: x: 2, y: 2, z: 4, core: 2. Of those that a mesh axis runs over, the one named last changes fastest.
Arguments:
- projection_input: bfloat16 [2, 2, 384, 4096], P('ckpt', 'groups', None, 'coord'), parts along dimension 1, may hold values from -6 to 6
- gate_output_gradient: bfloat16 [2, 2, 14336, 384], P('ckpt', 'groups', 'coord'), parts along dimension 1, may hold values from -0.59765625 to 0.59765625
- up_output_gradient: bfloat16 [2, 2, 14336, 384], P('ckpt', 'groups', 'coord'), parts along dimension 1, may hold values from -0.59765625 to 0.59765625
- hidden: bfloat16 [2, 2, 14336, 384], P('ckpt', 'groups', 'coord'), parts along dimension 1, may hold values from -6 to 6
- down_output_gradient: bfloat16 [2, 2, 384, 4096], P('ckpt', 'groups', None, 'coord'), parts along dimension 1, may hold values from -0.59765625 to 0.59765625
- gate_adapter_first: bfloat16 [2, 4096, 128], P('ckpt', 'coord'), may hold values from -0.09375 to 0.09375
- gate_adapter_second: bfloat16 [2, 14336, 128], P('ckpt', 'coord'), may hold values from -0.5 to 0.5
- up_adapter_first: bfloat16 [2, 4096, 128], P('ckpt', 'coord'), may hold values from -0.09375 to 0.09375
- up_adapter_second: bfloat16 [2, 14336, 128], P('ckpt', 'coord'), may hold values from -0.5 to 0.5
- down_adapter_first: bfloat16 [2, 14336, 128], P('ckpt', 'coord'), may hold values from -0.046875 to 0.046875
- down_adapter_second: bfloat16 [2, 4096, 128], P('ckpt', 'coord'), may hold values from -0.5 to 0.5
- random_sign_flags: int32 [16777216], P(('coord', 'ckpt')), may hold values 0 or 1
- sampled_coordinate_index: int32 [8192], replicated, may hold values from 0 to 16777215
Outputs:
- features: float32 [2, 8192], P('groups'), parts along dimension 0
There are 2 independent parts, one for each index of `groups`. A program takes and returns all parts, laid end to end along the dimension named above; an argument that names none is the same for every part. Nothing has to cross between parts.
All inputs are finite; a program needn't handle non-finite values. No bound on the sum of `random_sign_flags` on one device may be relied on, other than what follows from the above.
Results may differ from a plain program's by a relative error of at most 0.0031.
Values may be sent and summed in bfloat16 or wider, within the bound.
A program may use at most 64 MiB of HBM per device.

v0:
```python
import functools

import jax
import jax.numpy as jnp
from jax import lax
from jax.experimental import pallas as pl
from jax.experimental.pallas import tpu as pltpu
from jax.sharding import PartitionSpec as P

ADAPTER_SCALE = 2.0


def matrix_product(form, left, right):
    return jnp.einsum(form, left, right, preferred_element_type=jnp.float32)


def walsh_signs(rows, columns):
    shape = (rows, columns)
    i = lax.broadcasted_iota(jnp.int32, shape, 0)
    j = lax.broadcasted_iota(jnp.int32, shape, 1)
    return 1 - 2 * (lax.population_count(i & j) & 1)


def halves(value):
    high = value.astype(jnp.bfloat16)
    return high, (value - high.astype(jnp.float32)).astype(jnp.bfloat16)


def dot(left, right, dims=((1,), (0,))):
    return lax.dot_general(left, right, (dims, ((), ())), preferred_element_type=jnp.float32)


def butterflies(values):
    stride = 1
    while stride < len(values):
        result = list(values)
        for p in range(len(values)):
            if p & stride:
                continue
            a, b = values[p], values[p + stride]
            if b is None:
                result[p], result[p + stride] = a, a
            elif a is None:
                result[p], result[p + stride] = b, -b
            else:
                result[p], result[p + stride] = a + b, a - b
        values, stride = result, 2 * stride
    return values


def project_kernel(
    block_rows,
    chunk,
    row_ref,
    x_ref,
    gg_ref,
    gu_ref,
    h_ref,
    go_ref,
    products_ref,
    flags_ref,
    index_ref,
    out_ref,
    z_ref,
    picked_ref,
):
    total_rows, lanes = z_ref.shape
    width, deep = x_ref.shape[1], gg_ref.shape[0]
    gate_fwd, up_fwd, down_fwd, gate_back, up_back, down_back = range(6)

    row = 0
    for ref, which in ((x_ref, gate_back), (x_ref, up_back), (go_ref, down_fwd)):
        z_ref[pl.ds(row, width), :] = dot(ref[...], products_ref[which], ((0,), (0,)))
        row += width
    for ref, which in ((gg_ref, gate_fwd), (gu_ref, up_fwd), (h_ref, down_back)):
        z_ref[pl.ds(row, deep), :] = dot(ref[...], products_ref[which])
        row += deep
    filled = row
    count = total_rows // block_rows
    used = -(-filled // block_rows)
    if used * block_rows > filled:
        z_ref[pl.ds(filled, used * block_rows - filled), :] = jnp.zeros(
            (used * block_rows - filled, lanes), jnp.float32
        )

    lane_table = walsh_signs(lanes, lanes).astype(jnp.float32).astype(jnp.bfloat16)
    lane_table = jnp.concatenate([lane_table, lane_table], axis=0)
    row_table = walsh_signs(block_rows, block_rows).astype(jnp.float32).astype(jnp.bfloat16)
    row_table = jnp.concatenate([row_table, row_table], axis=1)

    def one_block(b, carry):
        rows = pl.ds(pl.multiple_of(b * block_rows, block_rows), block_rows)
        value = z_ref[rows, :]
        value = jnp.where(flags_ref[rows, :] != 0, -value, value)
        value = dot(jnp.concatenate(halves(value), axis=1), lane_table)
        value = dot(row_table, jnp.concatenate(halves(value), axis=0))
        z_ref[rows, :] = value
        return carry

    lax.fori_loop(0, used, one_block, 0, unroll=3 if used % 3 == 0 else 1)

    def across(r, carry):
        rows = [
            pl.ds(pl.multiple_of(b * block_rows + r * 8, 8), 8) for b in range(count)
        ]
        values = butterflies(
            [z_ref[rows[b], :] if b < used else None for b in range(count)]
        )
        for b in range(count):
            z_ref[rows[b], :] = values[b]
        return carry

    lax.fori_loop(0, block_rows // 8, across, 0)

    def pick(t, carry):
        for k in range(chunk):
            picked_ref[pl.ds(k, 1), :] = z_ref[pl.ds(row_ref[t * chunk + k], 1), :]
        columns = index_ref[pl.ds(t, 1), :] & (lanes - 1)
        turned = picked_ref[...].T
        here = lax.broadcasted_iota(jnp.int32, (lanes, chunk), 0) == columns
        out_ref[pl.ds(t, 1), :] = jnp.sum(jnp.where(here, turned, 0.0), axis=0, keepdims=True)
        return carry

    lax.fori_loop(0, index_ref.shape[0], pick, 0)


def project(x, gg, gu, h, go, products, flags, index):
    lanes = products.shape[2]
    chunk = 128
    total_rows = flags.shape[0] // lanes
    block_rows = min(256, total_rows)
    tiles = index.shape[0] // chunk
    row_of = (index // lanes) % total_rows
    vmem = pl.BlockSpec(memory_space=pltpu.VMEM)
    return pl.pallas_call(
        functools.partial(project_kernel, block_rows, chunk),
        out_shape=jax.ShapeDtypeStruct((tiles, chunk), jnp.float32),
        in_specs=[pl.BlockSpec(memory_space=pltpu.SMEM)] + [vmem] * 8,
        out_specs=vmem,
        scratch_shapes=[
            pltpu.VMEM((total_rows, lanes), jnp.float32),
            pltpu.VMEM((chunk, lanes), jnp.float32),
        ],
        compiler_params=pltpu.CompilerParams(vmem_limit_bytes=48 * 1024 * 1024),
    )(row_of, x, gg, gu, h, go, products, flags.reshape(total_rows, lanes), index.reshape(tiles, chunk))


def shards(
    projection_input,
    gate_output_gradient,
    up_output_gradient,
    hidden,
    down_output_gradient,
    gate_adapter_first,
    gate_adapter_second,
    up_adapter_first,
    up_adapter_second,
    down_adapter_first,
    down_adapter_second,
    random_sign_flags,
    sampled_coordinate_index,
):
    x, go = projection_input[0, 0], down_output_gradient[0, 0]
    gg, gu, h = gate_output_gradient[0, 0], up_output_gradient[0, 0], hidden[0, 0]
    partials = jnp.stack(
        [
            matrix_product("uj,jx->ux", x, gate_adapter_first[0]),
            matrix_product("uj,jx->ux", x, up_adapter_first[0]),
            matrix_product("do,da->oa", h, down_adapter_first[0]),
            matrix_product("do,da->oa", gg, gate_adapter_second[0]),
            matrix_product("do,da->oa", gu, up_adapter_second[0]),
            matrix_product("uj,jx->ux", go, down_adapter_second[0]),
        ]
    )
    products = lax.psum(partials, "coord").astype(jnp.bfloat16)
    kept = project(x, gg, gu, h, go, products, random_sign_flags, sampled_coordinate_index)
    local_len = random_sign_flags.shape[0]
    block_count = lax.axis_size("coord") * lax.axis_size("ckpt")
    me = lax.axis_index("coord") * lax.axis_size("ckpt") + lax.axis_index("ckpt")
    parity = lax.population_count((sampled_coordinate_index // local_len) & me) & 1
    scale = ADAPTER_SCALE * float(local_len * block_count) ** (-0.5)
    kept = jnp.where(parity.reshape(kept.shape) != 0, -scale, scale) * kept
    return lax.psum(kept, ("coord", "ckpt")).reshape(1, -1)


def solution(mesh):
    in_specs = (
        P("ckpt", "groups", None, "coord"),
        P("ckpt", "groups", "coord", None),
        P("ckpt", "groups", "coord", None),
        P("ckpt", "groups", "coord", None),
        P("ckpt", "groups", None, "coord"),
        P("ckpt", "coord", None),
        P("ckpt", "coord", None),
        P("ckpt", "coord", None),
        P("ckpt", "coord", None),
        P("ckpt", "coord", None),
        P("ckpt", "coord", None),
        P(("coord", "ckpt")),
        P(),
    )
    out_specs = P("groups", None)
    return jax.shard_map(shards, mesh=mesh, in_specs=in_specs, out_specs=out_specs, check_vma=False)
```

profile of v0, /device:TPU:0, one launch (start us, length us, event | category | flops | bytes accessed | tf_op | source)
XLA Modules:
  0.0 174.4 jit_solution(12279141458440918979)
XLA Ops:
  0.0 0.0 copy-start
  0.0 0.0 copy-start.3
  0.0 2.1 %fusion.2 = f32[6,384,128]{2,1,0:T(8,128)} fusion(bf16[1,512,128]{2,1,0:T(8,128)(2,1)} %param.18, bf16[1,1,384,512]{3,2,1,0:T(8,128)(2,1)} %param.13), kind=kOutput, calls=%fused_computation.5 | convolution fusion | flops 50331648 | bytes 720896 | tf_op jit(solution)/shard_map/uj,jx->ux/dot_general | solution.py:14
  2.1 2.0 %fusion.1 = f32[6,384,128]{2,1,0:T(8,128)} fusion(f32[6,384,128]{2,1,0:T(8,128)} %fusion.2, bf16[1,512,128]{2,1,0:T(8,128)(2,1)} %param.20, bf16[1,1,384,512]{3,2,1,0:T(8,128)(2,1)} %param.13), kind=kOutput, calls=%fused_computation.3 | convolution fusion | flops 50331648 | bytes 720896 | tf_op jit(solution)/shard_map/uj,jx->ux/dot_general | solution.py:14
  4.0 0.0 copy-done
  4.1 0.0 copy-done.3
  4.1 0.0 copy-start.1
  4.1 0.0 copy-start.10
  4.1 1.2 fusion.5
  5.3 0.1 copy-done.1
  5.4 0.1 copy-done.10
  5.5 0.0 copy-start.2
  5.5 0.0 copy-start.11
  5.5 1.2 fusion.4
  6.7 0.1 copy-done.2
  6.8 0.1 copy-done.11
  6.9 0.0 copy-start.7
  6.9 0.0 copy-start.12
  6.9 1.2 fusion.3
  8.2 0.0 copy-done.7
  8.2 0.0 copy-done.12
  8.2 0.0 copy-start.9
  8.2 0.9 fusion
  9.1 76.3 %all-reduce.1.products_ref = bf16[6,384,128]{2,1,0:T(8,128)(2,1)} all-reduce(f32[6,384,128]{2,1,0:T(8,128)} %fusion), channel_id=1, replica_groups=mesh['groups'=2,'coord'=8,'ckpt'=2] {'coord'}, use_global_device_ids=true, to_apply=%region_0.0 | all-reduce | flops 294912 | bytes 1769472 | tf_op jit(solution)/shard_map/psum | solution.py:175
  85.4 0.0 copy-done.9
  85.4 0.0 copy-start.4
  85.4 1.3 copy-done.4
  86.8 0.0 copy-start.5
  86.8 1.0 copy-done.5
  87.8 0.0 copy-start.6
  87.8 1.1 copy-done.6
  88.8 0.0 copy-start.8
  88.8 1.0 copy-done.8
  89.8 26.3 %shard_map.127 = f32[64,128]{1,0:T(8,128)S(1)} custom-call(s32[8192]{0:T(1024)S(1)} %add_select_fusion.row_ref, bf16[384,512]{1,0:T(8,128)(2,1)S(1)} %bitcast.67, bf16[1792,384]{1,0:T(8,128)(2,1)S(1)} %bitcast.64, bf16[1792,384]{1,0:T(8,128)(2,1)S(1)} %bitcast.65, bf16[1792,384]{1,0:T(8,128)(2,1)S(1)} %bitcast.66, bf16[384,512]{1,0:T(8,128)(2,1)S(1)} %bitcast.68, ...), custom_call_target="tpu_custom_call" | custom-call | tf_op jit(solution)/shard_map/pallas_call | solution.py:135
  116.2 58.2 %psum.15 = f32[1,8192]{1,0:T(1,128)} all-reduce(f32[1,8192]{1,0:T(1,128)S(1)} %bitcast.71), channel_id=1, replica_groups=mesh['groups'=2,'coord'=8,'ckpt'=2] {'coord','ckpt'}, use_global_device_ids=true, to_apply=%region_1.2 | all-reduce | flops 8192 | bytes 65536 | tf_op jit(solution)/shard_map/psum | solution.py:183
  (2 shorter events, 0.1 us)
Async XLA Ops:
  0.0 4.0 %copy-start = (bf16[1,1792,128]{2,1,0:T(8,128)(2,1)S(1)}, bf16[1,1792,128]{2,1,0:T(8,128)(2,1)}, u32[]{:S(2)}) copy-start(bf16[1,1792,128]{2,1,0:T(8,128)(2,1)} %param.22) | copy-start | bytes 1376260
  0.0 4.0 %copy-start.3 = (bf16[1,1,1792,384]{3,2,1,0:T(8,128)(2,1)S(1)}, bf16[1,1,1792,384]{3,2,1,0:T(8,128)(2,1)}, u32[]{:S(2)}) copy-start(bf16[1,1,1792,384]{3,2,1,0:T(8,128)(2,1)} %param.16) | copy-start | bytes 4128772
  4.1 1.3 copy-start.1
  4.1 1.4 copy-start.10
  5.5 1.3 copy-start.2
  5.5 1.4 copy-start.11
  6.9 1.2 copy-start.7
  6.9 1.2 copy-start.12
  8.2 77.2 %copy-start.9 = (s32[8192]{0:T(1024)S(1)}, s32[8192]{0:T(1024)}, u32[]{:S(2)}) copy-start(s32[8192]{0:T(1024)} %param.25) | copy-start | bytes 98308
  85.4 1.3 copy-start.4
  86.8 1.0 copy-start.5
  87.8 1.1 copy-start.6
  88.8 1.0 copy-start.8
where the time goes:
time: 175 us; the launch traced here: 174 us
  blocking collectives  134 us (77%)
  Pallas kernels  26.3 us (15%)
  matrix products  8.71 us (5%)
  local copies, waits for them, and re-layouts  4.77 us (3%)
    psum x1, blocking collectives, shards(): products = lax.psum(partials, 'coord').astype(jnp.bfloat16)  76.3 us
    psum x1, blocking collectives, shards(): return lax.psum(kept, ('coord', 'ckpt')).reshape(1, -1)  58.2 us
    pallas_call x1, Pallas kernels, project(): pl.pallas_call(functools.partial(project_kernel, block_rows, chunk), out_...  26.3 us
    dot_general x6, matrix products, matrix_product(): return jnp.einsum(form, left, right, preferred_element_type=jnp.float32)  8.71 us
    unnamed x26, local copies, waits for them, and re-layouts  4.77 us

commit v1 on v0

--- a/solution.py
+++ b/solution.py
@@ -145,6 +145,181 @@
     )(row_of, x, gg, gu, h, go, products, flags.reshape(total_rows, lanes), index.reshape(tiles, chunk))
 
 
+MESH = pl.DeviceIdType.MESH
+
+
+def greet(peers):
+    barrier = pltpu.get_barrier_semaphore()
+    for peer in peers:
+        pl.semaphore_signal(barrier, inc=1, device_id=peer, device_id_type=MESH)
+    return lambda: pl.semaphore_wait(barrier, len(peers))
+
+
+def remote(source, target, send, receive, peer):
+    return pltpu.make_async_remote_copy(
+        src_ref=source,
+        dst_ref=target,
+        send_sem=send,
+        recv_sem=receive,
+        device_id=peer,
+        device_id_type=MESH,
+    )
+
+
+def products_kernel(
+    x_ref, gg_ref, gu_ref, h_ref, go_ref, a1, a2, a3, a4, a5, a6,
+    out_ref, part_ref, pair_ref, rest_ref,
+    send1, recv1, send2, recv2, send3, recv3, send4, recv4,
+):
+    count, two, outer, rows, lanes = part_ref.shape
+    me = lax.axis_index("coord")
+    mine, place = me % two, me // two
+    partner = {"coord": place * two + (1 - mine)}
+    others = [{"coord": (place + d) % outer * two + mine} for d in range(1, outer)]
+    wait_for_all = greet([partner] + others)
+
+    def first(i):
+        ref, weights, turned = (
+            (x_ref, a1, False),
+            (x_ref, a3, False),
+            (h_ref, a5, True),
+            (gg_ref, a2, True),
+            (gu_ref, a4, True),
+            (go_ref, a6, False),
+        )[i]
+        value = dot(ref[...], weights[...], ((0,), (0,)) if turned else ((1,), (0,)))
+        part_ref[i] = value.reshape(two, outer, rows, lanes)
+
+    def pair(i):
+        return remote(
+            part_ref.at[i, 1 - mine], pair_ref.at[i], send1.at[i], recv1.at[i], partner
+        )
+
+    def rest(i, d):
+        return remote(
+            part_ref.at[i, mine, (place + d) % outer],
+            rest_ref.at[i, d - 1],
+            send2.at[i, d - 1],
+            recv2.at[i, d - 1],
+            others[d - 1],
+        )
+
+    def spread(i, d):
+        block = out_ref.at[i, mine, place]
+        return remote(block, block, send3.at[i, d - 1], recv3.at[i, d - 1], others[d - 1])
+
+    def finish(i):
+        block = out_ref.at[i, mine]
+        return remote(block, block, send4.at[i], recv4.at[i], partner)
+
+    order = (0, 1, 5, 3, 4, 2)
+    lags = (0, 1, 2, 3)
+    for step in range(count + lags[3] + 1):
+        if step < count:
+            first(order[step])
+            if step == 0:
+                wait_for_all()
+            pair(order[step]).start()
+        if 0 <= step - lags[1] < count:
+            i = order[step - lags[1]]
+            pair(i).wait_recv()
+            part_ref[i, mine] += pair_ref[i]
+            for d in range(1, outer):
+                rest(i, d).start()
+        if 0 <= step - lags[2] < count:
+            i = order[step - lags[2]]
+            total = part_ref[i, mine, place]
+            for d in range(1, outer):
+                rest(i, d).wait_recv()
+                total = total + rest_ref[i, d - 1]
+            out_ref[i, mine, place] = total.astype(jnp.bfloat16)
+            for d in range(1, outer):
+                spread(i, d).start()
+        if 0 <= step - lags[3] < count:
+            i = order[step - lags[3]]
+            for d in range(1, outer):
+                spread(i, d).wait_recv()
+            finish(i).start()
+    for i in order:
+        finish(i).wait_recv()
+        pair(i).wait_send()
+        for d in range(1, outer):
+            rest(i, d).wait_send()
+            spread(i, d).wait_send()
+        finish(i).wait_send()
+
+
+def products_of(x, gg, gu, h, go, adapters, coord_count):
+    seq, lanes = x.shape[0], adapters[0].shape[1]
+    two, rows = 2, seq // coord_count
+    outer = coord_count // two
+    vmem = pl.BlockSpec(memory_space=pltpu.VMEM)
+    dma = pltpu.SemaphoreType.DMA
+    out = pl.pallas_call(
+        products_kernel,
+        out_shape=jax.ShapeDtypeStruct((6, two, outer, rows, lanes), jnp.bfloat16),
+        in_specs=[vmem] * 11,
+        out_specs=vmem,
+        scratch_shapes=[
+            pltpu.VMEM((6, two, outer, rows, lanes), jnp.float32),
+            pltpu.VMEM((6, outer, rows, lanes), jnp.float32),
+            pltpu.VMEM((6, outer - 1, rows, lanes), jnp.float32),
+            dma((6,)), dma((6,)),
+            dma((6, outer - 1)), dma((6, outer - 1)),
+            dma((6, outer - 1)), dma((6, outer - 1)),
+            dma((6,)), dma((6,)),
+        ],
+        compiler_params=pltpu.CompilerParams(
+            collective_id=0, has_side_effects=True, vmem_limit_bytes=40 * 1024 * 1024
+        ),
+    )(x, gg, gu, h, go, *adapters)
+    return out.reshape(6, seq, lanes)
+
+
+def total_kernel(members, kept_ref, out_ref, got_ref, send1, recv1, send2, recv2):
+    count = kept_ref.shape[0]
+    me = lax.axis_index("coord") * members + lax.axis_index("ckpt")
+    places = [(me + d) % count for d in range(1, count)]
+    peers = [{"coord": p // members, "ckpt": p % members} for p in places]
+    greet(peers)()
+    scatter = [
+        remote(kept_ref.at[places[d]], got_ref.at[d], send1.at[d], recv1.at[d], peers[d])
+        for d in range(count - 1)
+    ]
+    gather = [
+        remote(out_ref.at[me], out_ref.at[me], send2.at[d], recv2.at[d], peers[d])
+        for d in range(count - 1)
+    ]
+    for copy in scatter:
+        copy.start()
+    total = kept_ref[me]
+    for d, copy in enumerate(scatter):
+        copy.wait_recv()
+        total = total + got_ref[d]
+    out_ref[me] = total
+    for copy in gather:
+        copy.start()
+    for copy in gather:
+        copy.wait_recv()
+    for copy in scatter + gather:
+        copy.wait_send()
+
+
+def total_of(kept, count, members):
+    shape = (count, kept.size // count // 128, 128)
+    vmem = pl.BlockSpec(memory_space=pltpu.VMEM)
+    dma = pltpu.SemaphoreType.DMA
+    return pl.pallas_call(
+        functools.partial(total_kernel, members),
+        out_shape=jax.ShapeDtypeStruct(shape, jnp.float32),
+        in_specs=[vmem],
+        out_specs=vmem,
+        scratch_shapes=[pltpu.VMEM((count - 1,) + shape[1:], jnp.float32)]
+        + [dma((count - 1,))] * 4,
+        compiler_params=pltpu.CompilerParams(collective_id=1, has_side_effects=True),
+    )(kept.reshape(shape))
+
+
 def shards(
     projection_input,
     gate_output_gradient,
@@ -162,24 +337,41 @@
 ):
     x, go = projection_input[0, 0], down_output_gradient[0, 0]
     gg, gu, h = gate_output_gradient[0, 0], up_output_gradient[0, 0], hidden[0, 0]
-    partials = jnp.stack(
-        [
-            matrix_product("uj,jx->ux", x, gate_adapter_first[0]),
-            matrix_product("uj,jx->ux", x, up_adapter_first[0]),
-            matrix_product("do,da->oa", h, down_adapter_first[0]),
-            matrix_product("do,da->oa", gg, gate_adapter_second[0]),
-            matrix_product("do,da->oa", gu, up_adapter_second[0]),
-            matrix_product("uj,jx->ux", go, down_adapter_second[0]),
-        ]
-    )
-    products = lax.psum(partials, "coord").astype(jnp.bfloat16)
+    coord_count, members = lax.axis_size("coord"), lax.axis_size("ckpt")
+    adapters = [
+        adapter[0]
+        for adapter in (
+            gate_adapter_first,
+            gate_adapter_second,
+            up_adapter_first,
+            up_adapter_second,
+            down_adapter_first,
+            down_adapter_second,
+        )
+    ]
+    if coord_count % 2 == 0 and coord_count <= 32 and x.shape[0] % (16 * coord_count) == 0:
+        products = products_of(x, gg, gu, h, go, adapters, coord_count)
+    else:
+        partials = jnp.stack(
+            [
+                matrix_product("uj,jx->ux", x, adapters[0]),
+                matrix_product("uj,jx->ux", x, adapters[2]),
+                matrix_product("do,da->oa", h, adapters[4]),
+                matrix_product("do,da->oa", gg, adapters[1]),
+                matrix_product("do,da->oa", gu, adapters[3]),
+                matrix_product("uj,jx->ux", go, adapters[5]),
+            ]
+        )
+        products = lax.psum(partials, "coord").astype(jnp.bfloat16)
     kept = project(x, gg, gu, h, go, products, random_sign_flags, sampled_coordinate_index)
     local_len = random_sign_flags.shape[0]
-    block_count = lax.axis_size("coord") * lax.axis_size("ckpt")
-    me = lax.axis_index("coord") * lax.axis_size("ckpt") + lax.axis_index("ckpt")
+    block_count = coord_count * members
+    me = lax.axis_index("coord") * members + lax.axis_index("ckpt")
     parity = lax.population_count((sampled_coordinate_index // local_len) & me) & 1
     scale = ADAPTER_SCALE * float(local_len * block_count) ** (-0.5)
     kept = jnp.where(parity.reshape(kept.shape) != 0, -scale, scale) * kept
+    if block_count <= 32 and kept.size % (128 * block_count) == 0:
+        return total_of(kept, block_count, members).reshape(1, -1)
     return lax.psum(kept, ("coord", "ckpt")).reshape(1, -1)
 
 

time: 175 us -> 90.7 us (0.52)
  blocking collectives: 134 us -> 0 us
  Pallas kernels: 26.3 us -> 76.1 us
  matrix products: 8.71 us -> 0 us
  local copies, waits for them, and re-layouts: 4.77 us -> 13.2 us
    psum x2 -> x0, blocking collectives: 134 us -> none  [the longest x1 76.3 us: shards(): products = lax.psum(partials, 'coord').astype(jnp.bfloat16)]
    pallas_call x0 -> x2, Pallas kernels: none -> 49.8 us  [the longest x1 37.9 us: products_of(): pl.pallas_call(products_kernel, out_shape=jax.ShapeDtypeStruct((6, two, o...]
    dot_general x6 -> x0, matrix products: 8.71 us -> none  [matrix_product(): return jnp.einsum(form, left, right, preferred_element_type=jnp.float32)]
    unnamed x26 -> x35, local copies, waits for them, and re-layouts: 4.77 us -> 13.2 us
where the time goes in v1:
time: 90.7 us; the launch traced here: 90 us
  Pallas kernels  76.1 us (84%)
  local copies, waits for them, and re-layouts  13.2 us (15%)
    pallas_call x1, Pallas kernels, products_of(): pl.pallas_call(products_kernel, out_shape=jax.ShapeDtypeStruct((6, two, o...  37.9 us
    pallas_call x1, Pallas kernels, project(): pl.pallas_call(functools.partial(project_kernel, block_rows, chunk), out_...  26.3 us
    unnamed x35, local copies, waits for them, and re-layouts  13.2 us
    pallas_call x1, Pallas kernels, total_of(): pl.pallas_call(functools.partial(total_kernel, members), out_shape=jax.Sh...  11.9 us

profile of v1, /device:TPU:0, one launch (start us, length us, event | category | flops | bytes accessed | tf_op | source)
XLA Modules:
  0.0 90.0 jit_solution(12638722636902751503)
XLA Ops:
  0.0 0.0 copy-start
  0.0 1.3 %copy-done = bf16[1,1,1792,384]{3,2,1,0:T(8,128)(2,1)S(1)} copy-done((bf16[1,1,1792,384]{3,2,1,0:T(8,128)(2,1)S(1)}, bf16[1,1,1792,384]{3,2,1,0:T(8,128)(2,1)}, u32[]{:S(2)}) %copy-start) | copy-done | bytes 1376280
  1.3 0.0 copy-start.2
  1.3 1.3 %copy-done.2 = bf16[1,1,1792,384]{3,2,1,0:T(8,128)(2,1)S(1)} copy-done((bf16[1,1,1792,384]{3,2,1,0:T(8,128)(2,1)S(1)}, bf16[1,1,1792,384]{3,2,1,0:T(8,128)(2,1)}, u32[]{:S(2)}) %copy-start.2) | copy-done | bytes 1376280
  2.7 0.0 copy-start.4
  2.7 1.3 %copy-done.4 = bf16[1,1,1792,384]{3,2,1,0:T(8,128)(2,1)S(1)} copy-done((bf16[1,1,1792,384]{3,2,1,0:T(8,128)(2,1)S(1)}, bf16[1,1,1792,384]{3,2,1,0:T(8,128)(2,1)}, u32[]{:S(2)}) %copy-start.4) | copy-done | bytes 1376280
  4.0 0.0 copy-start.6
  4.0 1.0 %copy-done.6 = bf16[1,1,384,512]{3,2,1,0:T(8,128)(2,1)S(1)} copy-done((bf16[1,1,384,512]{3,2,1,0:T(8,128)(2,1)S(1)}, bf16[1,1,384,512]{3,2,1,0:T(8,128)(2,1)}, u32[]{:S(2)}) %copy-start.6) | copy-done | bytes 393240
  5.0 0.0 copy-start.8
  5.0 1.0 %copy-done.8 = bf16[1,1,384,512]{3,2,1,0:T(8,128)(2,1)S(1)} copy-done((bf16[1,1,384,512]{3,2,1,0:T(8,128)(2,1)S(1)}, bf16[1,1,384,512]{3,2,1,0:T(8,128)(2,1)}, u32[]{:S(2)}) %copy-start.8) | copy-done | bytes 393240
  6.0 0.0 copy-start.10
  6.0 1.0 %copy-done.10 = bf16[1,1792,128]{2,1,0:T(8,128)(2,1)S(1)} copy-done((bf16[1,1792,128]{2,1,0:T(8,128)(2,1)S(1)}, bf16[1,1792,128]{2,1,0:T(8,128)(2,1)}, u32[]{:S(2)}) %copy-start.10) | copy-done | bytes 458776
  7.0 0.0 copy-start.11
  7.0 1.0 %copy-done.11 = bf16[1,1792,128]{2,1,0:T(8,128)(2,1)S(1)} copy-done((bf16[1,1792,128]{2,1,0:T(8,128)(2,1)S(1)}, bf16[1,1792,128]{2,1,0:T(8,128)(2,1)}, u32[]{:S(2)}) %copy-start.11) | copy-done | bytes 458776
  8.0 0.0 copy-start.12
  8.1 1.0 %copy-done.12 = bf16[1,1792,128]{2,1,0:T(8,128)(2,1)S(1)} copy-done((bf16[1,1792,128]{2,1,0:T(8,128)(2,1)S(1)}, bf16[1,1792,128]{2,1,0:T(8,128)(2,1)}, u32[]{:S(2)}) %copy-start.12) | copy-done | bytes 458776
  9.1 0.0 copy-start.14
  9.1 0.9 %copy-done.14 = bf16[1,512,128]{2,1,0:T(8,128)(2,1)S(1)} copy-done((bf16[1,512,128]{2,1,0:T(8,128)(2,1)S(1)}, bf16[1,512,128]{2,1,0:T(8,128)(2,1)}, u32[]{:S(2)}) %copy-start.14) | copy-done | bytes 131096
  10.0 0.0 copy-start.15
  10.0 0.9 %copy-done.15 = bf16[1,512,128]{2,1,0:T(8,128)(2,1)S(1)} copy-done((bf16[1,512,128]{2,1,0:T(8,128)(2,1)S(1)}, bf16[1,512,128]{2,1,0:T(8,128)(2,1)}, u32[]{:S(2)}) %copy-start.15) | copy-done | bytes 131096
  10.9 0.0 copy-start.16
  10.9 0.9 %copy-done.16 = bf16[1,512,128]{2,1,0:T(8,128)(2,1)S(1)} copy-done((bf16[1,512,128]{2,1,0:T(8,128)(2,1)S(1)}, bf16[1,512,128]{2,1,0:T(8,128)(2,1)}, u32[]{:S(2)}) %copy-start.16) | copy-done | bytes 131096
  11.8 0.0 copy-start.13
  11.8 0.0 copy-start.1
  11.8 0.0 copy-start.3
  11.8 0.0 copy-start.5
  11.8 0.0 copy-start.7
  11.8 0.0 copy-start.9
  11.8 37.9 %shard_map.127 = bf16[6,2,4,48,128]{4,3,2,1,0:T(8,128)(2,1)S(1)} custom-call(bf16[384,512]{1,0:T(8,128)(2,1)S(1)} %bitcast.25, bf16[1792,384]{1,0:T(8,128)(2,1)S(1)} %bitcast.18, bf16[1792,384]{1,0:T(8,128)(2,1)S(1)} %bitcast.20, bf16[1792,384]{1,0:T(8,128)(2,1)S(1)} %bitcast.22, bf16[384,512]{1,0:T(8,128)(2,1)S(1)} %bitcast.27, ...), custom_call_target="tpu_custom_call" | custom-call | tf_op jit(solution)/shard_map/pallas_call | solution.py:258
  49.7 0.0 copy-done.13
  49.8 0.0 copy-done.1
  49.8 0.0 copy-done.3
  49.8 0.0 copy-done.5
  49.8 0.0 copy-done.7
  49.8 0.0 copy-done.9
  49.8 26.3 %shard_map.128 = f32[64,128]{1,0:T(8,128)S(1)} custom-call(s32[8192]{0:T(1024)S(1)} %add_select_fusion.row_ref, bf16[384,512]{1,0:T(8,128)(2,1)S(1)} %bitcast.26, bf16[1792,384]{1,0:T(8,128)(2,1)S(1)} %bitcast.19, bf16[1792,384]{1,0:T(8,128)(2,1)S(1)} %bitcast.21, bf16[1792,384]{1,0:T(8,128)(2,1)S(1)} %bitcast.23, bf16[384,512]{1,0:T(8,128)(2,1)S(1)} %bitcast.28, ...), custom_call_target="tpu_custom_call" | custom-call | tf_op jit(solution)/shard_map/pallas_call | solution.py:135
  76.1 0.6 bitcast_multiply_fusion
  76.8 11.9 %shard_map.129 = f32[16,4,128]{2,1,0:T(4,128)} custom-call(f32[16,4,128]{2,1,0:T(4,128)} %bitcast.37), custom_call_target="tpu_custom_call" | custom-call | tf_op jit(solution)/shard_map/pallas_call | solution.py:312
  88.7 1.4 %copy.15 = f32[1,8192]{1,0:T(1,128)} copy(f32[1,8192]{1,0:T(1,128)} %bitcast.38) | data formatting | bytes 65536
  (1 shorter events, 0.0 us)
Async XLA Ops:
  0.0 1.3 %copy-start = (bf16[1,1,1792,384]{3,2,1,0:T(8,128)(2,1)S(1)}, bf16[1,1,1792,384]{3,2,1,0:T(8,128)(2,1)}, u32[]{:S(2)}) copy-start(bf16[1,1,1792,384]{3,2,1,0:T(8,128)(2,1)} %param.14) | copy-start | bytes 4128772
  1.3 1.3 %copy-start.2 = (bf16[1,1,1792,384]{3,2,1,0:T(8,128)(2,1)S(1)}, bf16[1,1,1792,384]{3,2,1,0:T(8,128)(2,1)}, u32[]{:S(2)}) copy-start(bf16[1,1,1792,384]{3,2,1,0:T(8,128)(2,1)} %param.15) | copy-start | bytes 4128772
  2.7 1.3 %copy-start.4 = (bf16[1,1,1792,384]{3,2,1,0:T(8,128)(2,1)S(1)}, bf16[1,1,1792,384]{3,2,1,0:T(8,128)(2,1)}, u32[]{:S(2)}) copy-start(bf16[1,1,1792,384]{3,2,1,0:T(8,128)(2,1)} %param.16) | copy-start | bytes 4128772
  4.0 1.0 %copy-start.6 = (bf16[1,1,384,512]{3,2,1,0:T(8,128)(2,1)S(1)}, bf16[1,1,384,512]{3,2,1,0:T(8,128)(2,1)}, u32[]{:S(2)}) copy-start(bf16[1,1,384,512]{3,2,1,0:T(8,128)(2,1)} %param.13) | copy-start | bytes 1179652
  5.0 1.0 %copy-start.8 = (bf16[1,1,384,512]{3,2,1,0:T(8,128)(2,1)S(1)}, bf16[1,1,384,512]{3,2,1,0:T(8,128)(2,1)}, u32[]{:S(2)}) copy-start(bf16[1,1,384,512]{3,2,1,0:T(8,128)(2,1)} %param.17) | copy-start | bytes 1179652
  6.0 1.0 %copy-start.10 = (bf16[1,1792,128]{2,1,0:T(8,128)(2,1)S(1)}, bf16[1,1792,128]{2,1,0:T(8,128)(2,1)}, u32[]{:S(2)}) copy-start(bf16[1,1792,128]{2,1,0:T(8,128)(2,1)} %param.19) | copy-start | bytes 1376260
  7.0 1.0 %copy-start.11 = (bf16[1,1792,128]{2,1,0:T(8,128)(2,1)S(1)}, bf16[1,1792,128]{2,1,0:T(8,128)(2,1)}, u32[]{:S(2)}) copy-start(bf16[1,1792,128]{2,1,0:T(8,128)(2,1)} %param.21) | copy-start | bytes 1376260
  8.0 1.0 %copy-start.12 = (bf16[1,1792,128]{2,1,0:T(8,128)(2,1)S(1)}, bf16[1,1792,128]{2,1,0:T(8,128)(2,1)}, u32[]{:S(2)}) copy-start(bf16[1,1792,128]{2,1,0:T(8,128)(2,1)} %param.22) | copy-start | bytes 1376260
  9.1 0.9 %copy-start.14 = (bf16[1,512,128]{2,1,0:T(8,128)(2,1)S(1)}, bf16[1,512,128]{2,1,0:T(8,128)(2,1)}, u32[]{:S(2)}) copy-start(bf16[1,512,128]{2,1,0:T(8,128)(2,1)} %param.18) | copy-start | bytes 393220
  10.0 0.9 %copy-start.15 = (bf16[1,512,128]{2,1,0:T(8,128)(2,1)S(1)}, bf16[1,512,128]{2,1,0:T(8,128)(2,1)}, u32[]{:S(2)}) copy-start(bf16[1,512,128]{2,1,0:T(8,128)(2,1)} %param.20) | copy-start | bytes 393220
  10.9 0.9 %copy-start.16 = (bf16[1,512,128]{2,1,0:T(8,128)(2,1)S(1)}, bf16[1,512,128]{2,1,0:T(8,128)(2,1)}, u32[]{:S(2)}) copy-start(bf16[1,512,128]{2,1,0:T(8,128)(2,1)} %param.23) | copy-start | bytes 393220
  11.8 38.0 %copy-start.13 = (s32[8192]{0:T(1024)S(1)}, s32[8192]{0:T(1024)}, u32[]{:S(2)}) copy-start(s32[8192]{0:T(1024)} %param.25) | copy-start | bytes 98308
  11.8 38.0 %copy-start.1 = (bf16[1,1,1792,384]{3,2,1,0:T(8,128)(2,1)S(1)}, bf16[1,1,1792,384]{3,2,1,0:T(8,128)(2,1)}, u32[]{:S(2)}) copy-start(bf16[1,1,1792,384]{3,2,1,0:T(8,128)(2,1)} %param.14) | copy-start | bytes 4128772
  11.8 38.0 %copy-start.3 = (bf16[1,1,1792,384]{3,2,1,0:T(8,128)(2,1)S(1)}, bf16[1,1,1792,384]{3,2,1,0:T(8,128)(2,1)}, u32[]{:S(2)}) copy-start(bf16[1,1,1792,384]{3,2,1,0:T(8,128)(2,1)} %param.15) | copy-start | bytes 4128772
  11.8 38.0 %copy-start.5 = (bf16[1,1,1792,384]{3,2,1,0:T(8,128)(2,1)S(1)}, bf16[1,1,1792,384]{3,2,1,0:T(8,128)(2,1)}, u32[]{:S(2)}) copy-start(bf16[1,1,1792,384]{3,2,1,0:T(8,128)(2,1)} %param.16) | copy-start | bytes 4128772
  11.8 38.0 %copy-start.7 = (bf16[1,1,384,512]{3,2,1,0:T(8,128)(2,1)S(1)}, bf16[1,1,384,512]{3,2,1,0:T(8,128)(2,1)}, u32[]{:S(2)}) copy-start(bf16[1,1,384,512]{3,2,1,0:T(8,128)(2,1)} %param.13) | copy-start | bytes 1179652
  11.8 38.0 %copy-start.9 = (bf16[1,1,384,512]{3,2,1,0:T(8,128)(2,1)S(1)}, bf16[1,1,384,512]{3,2,1,0:T(8,128)(2,1)}, u32[]{:S(2)}) copy-start(bf16[1,1,384,512]{3,2,1,0:T(8,128)(2,1)} %param.17) | copy-start | bytes 1179652

commit v2 on v0

--- a/solution.py
+++ b/solution.py
@@ -145,6 +145,289 @@
     )(row_of, x, gg, gu, h, go, products, flags.reshape(total_rows, lanes), index.reshape(tiles, chunk))
 
 
+MESH = pl.DeviceIdType.MESH
+
+
+def greet(peers):
+    barrier = pltpu.get_barrier_semaphore()
+    for peer in peers:
+        pl.semaphore_signal(barrier, inc=1, device_id=peer, device_id_type=MESH)
+    return lambda: pl.semaphore_wait(barrier, len(peers))
+
+
+def remote(source, target, send, receive, peer):
+    return pltpu.make_async_remote_copy(
+        src_ref=source,
+        dst_ref=target,
+        send_sem=send,
+        recv_sem=receive,
+        device_id=peer,
+        device_id_type=MESH,
+    )
+
+def fused_kernel(
+    members, block_rows, row_ref, *refs
+):
+    hbm, (sums_ref,), scratch = refs[:13], refs[13:14], refs[14:]
+    local, scratch = scratch[:13], scratch[13:]
+    (
+        part_ref, pair_ref, rest_ref, out_ref, z_ref, picked_ref, kept_ref, got_ref,
+        load, send1, recv1, send2, recv2, send3, recv3, send4, recv4, send5, recv5, send6, recv6,
+    ) = scratch
+    x_ref, gg_ref, gu_ref, h_ref, go_ref, a1, a2, a3, a4, a5, a6, flags_ref, index_ref = local
+    count, two, outer, rows, lanes = part_ref.shape
+    members_all = kept_ref.shape[0]
+    coord = lax.axis_index("coord")
+    mine, place = coord % two, coord // two
+    flat = coord * members + lax.axis_index("ckpt")
+
+    loads = [pltpu.make_async_copy(hbm[n], local[n], load.at[n]) for n in range(13)]
+    for n in (0, 5, 7, 4, 10, 1, 6, 2, 8, 3, 9, 11, 12):
+        loads[n].start()
+
+    def member(d):
+        p = (flat + d) % members_all
+        return {"coord": p // members, "ckpt": p % members}
+
+    wait_for_all = greet([member(d) for d in range(1, members_all)])
+    partner = {"coord": place * two + (1 - mine)}
+    others = [{"coord": (place + d) % outer * two + mine} for d in range(1, outer)]
+
+    def first(i):
+        n, m, turned = (
+            (0, 5, False),
+            (0, 7, False),
+            (3, 9, True),
+            (1, 6, True),
+            (2, 8, True),
+            (4, 10, False),
+        )[i]
+        if i != 1:
+            loads[n].wait()
+        loads[m].wait()
+        value = dot(local[n][...], local[m][...], ((0,), (0,)) if turned else ((1,), (0,)))
+        part_ref[i] = value.reshape(two, outer, rows, lanes)
+
+    def pair(i):
+        return remote(
+            part_ref.at[i, 1 - mine], pair_ref.at[i], send1.at[i], recv1.at[i], partner
+        )
+
+    def rest(i, d):
+        return remote(
+            part_ref.at[i, mine, (place + d) % outer],
+            rest_ref.at[i, d - 1],
+            send2.at[i, d - 1],
+            recv2.at[i, d - 1],
+            others[d - 1],
+        )
+
+    def spread(i, d):
+        block = out_ref.at[i, mine, place]
+        return remote(block, block, send3.at[i, d - 1], recv3.at[i, d - 1], others[d - 1])
+
+    def finish(i):
+        block = out_ref.at[i, mine]
+        return remote(block, block, send4.at[i], recv4.at[i], partner)
+
+    def scatter_products(i):
+        pair(i).wait_recv()
+        part_ref[i, mine] += pair_ref[i]
+        for d in range(1, outer):
+            rest(i, d).start()
+
+    def sum_products(i):
+        total = part_ref[i, mine, place]
+        for d in range(1, outer):
+            rest(i, d).wait_recv()
+            total = total + rest_ref[i, d - 1]
+        out_ref[i, mine, place] = total.astype(jnp.bfloat16)
+        for d in range(1, outer):
+            spread(i, d).start()
+
+    def finish_products(i):
+        for d in range(1, outer):
+            spread(i, d).wait_recv()
+        finish(i).start()
+
+    lane_table = walsh_signs(lanes, lanes).astype(jnp.float32).astype(jnp.bfloat16)
+    lane_table = jnp.concatenate([lane_table, lane_table], axis=0)
+    row_table = walsh_signs(block_rows, block_rows).astype(jnp.float32).astype(jnp.bfloat16)
+    row_table = jnp.concatenate([row_table, row_table], axis=1)
+    width, deep = x_ref.shape[1], gg_ref.shape[0]
+
+    def transform(b):
+        span = pl.ds(pl.multiple_of(b * block_rows, block_rows), block_rows)
+        value = z_ref[span, :]
+        value = jnp.where(flags_ref[span, :] != 0, -value, value)
+        value = dot(jnp.concatenate(halves(value), axis=1), lane_table)
+        return span, dot(row_table, jnp.concatenate(halves(value), axis=0))
+
+    def gradient(i):
+        finish(i).wait_recv()
+        right = out_ref[i].reshape(two * outer * rows, lanes)
+        ref, turned, row = (
+            (gg_ref, False, 3 * width),
+            (gu_ref, False, 3 * width + deep),
+            (go_ref, True, 2 * width),
+            (x_ref, True, 0),
+            (x_ref, True, width),
+            (h_ref, False, 3 * width + 2 * deep),
+        )[i]
+        size = width if turned else deep
+        z_ref[pl.ds(row, size), :] = dot(ref[...], right, ((0,), (0,)) if turned else ((1,), (0,)))
+        start, blocks = row // block_rows, size // block_rows
+
+        def some(n, at):
+            done = [transform(at + k) for k in range(n)]
+            for span, value in done:
+                z_ref[span, :] = value
+
+        if blocks >= 2:
+
+            def step(g, carry):
+                some(2, start + 2 * g)
+                return carry
+
+            lax.fori_loop(0, blocks // 2, step, 0)
+        if blocks % 2:
+            some(1, start + blocks - 1)
+
+    order = (0, 1, 5, 3, 4, 2)
+    for n, i in enumerate(order):
+        first(i)
+        if n == 0:
+            wait_for_all()
+        pair(i).start()
+    for i in order:
+        scatter_products(i)
+    for n, i in enumerate(order):
+        sum_products(i)
+        if n >= 2:
+            finish_products(order[n - 2])
+    loads[11].wait()
+    finish_products(order[4])
+    gradient(order[0])
+    finish_products(order[5])
+    for i in order[1:]:
+        gradient(i)
+
+    filled = 3 * (width + deep) // block_rows
+    total_blocks = z_ref.shape[0] // block_rows
+
+    def across(r, carry):
+        spans = [
+            pl.ds(pl.multiple_of(b * block_rows + r * 8, 8), 8) for b in range(total_blocks)
+        ]
+        values = butterflies(
+            [z_ref[spans[b], :] if b < filled else None for b in range(total_blocks)]
+        )
+        for b in range(total_blocks):
+            z_ref[spans[b], :] = values[b]
+        return carry
+
+    lax.fori_loop(0, block_rows // 8, across, 0)
+
+    loads[12].wait()
+    tiles, chunk = kept_ref.shape[1:]
+    local_len = z_ref.shape[0] * lanes
+    here = lax.broadcasted_iota(jnp.int32, (lanes, chunk), 0)
+
+    def pick(j):
+        for q in range(tiles):
+            t = j * tiles + q
+            for k in range(chunk):
+                picked_ref[q, pl.ds(k, 1), :] = z_ref[pl.ds(row_ref[t * chunk + k], 1), :]
+            index = index_ref[pl.ds(j, 1), q, :]
+            chosen = jnp.where(here == (index & (lanes - 1)), picked_ref[q].T, 0.0)
+            chosen = jnp.sum(chosen, axis=0, keepdims=True)
+            odd = lax.population_count((index // local_len) & flat) & 1
+            kept_ref[pl.ds(j, 1), q, :] = jnp.where(odd != 0, -chosen, chosen)
+
+    def scatter(d):
+        return remote(
+            kept_ref.at[(flat + d) % members_all],
+            got_ref.at[d - 1],
+            send5.at[d - 1],
+            recv5.at[d - 1],
+            member(d),
+        )
+
+    def gather(d):
+        return remote(
+            sums_ref.at[flat], sums_ref.at[flat], send6.at[d - 1], recv6.at[d - 1], member(d)
+        )
+
+    def pick_and_send(d, carry):
+        pick((flat + d) % members_all)
+
+        @pl.when(d < members_all)
+        def _():
+            scatter(d).start()
+
+        return carry
+
+    lax.fori_loop(1, members_all + 1, pick_and_send, 0)
+    total = kept_ref[flat]
+    for d in range(1, members_all):
+        scatter(d).wait_recv()
+        total = total + got_ref[d - 1]
+    sums_ref[flat] = total
+    for d in range(1, members_all):
+        gather(d).start()
+    for i in order:
+        pair(i).wait_send()
+        for d in range(1, outer):
+            rest(i, d).wait_send()
+            spread(i, d).wait_send()
+        finish(i).wait_send()
+    for d in range(1, members_all):
+        gather(d).wait_recv()
+        scatter(d).wait_send()
+        gather(d).wait_send()
+
+
+def fused(x, gg, gu, h, go, adapters, flags, index, coord_count, members):
+    seq, lanes = x.shape[0], adapters[0].shape[1]
+    chunk, block_rows = 128, 256
+    total_rows = flags.shape[0] // lanes
+    two, rows = 2, seq // coord_count
+    outer, everyone = coord_count // two, coord_count * members
+    shape = (everyone, index.shape[0] // (everyone * chunk), chunk)
+    row_of = (index // lanes) % total_rows
+    vmem = pl.BlockSpec(memory_space=pltpu.VMEM)
+    dma = pltpu.SemaphoreType.DMA
+    arrays = (x, gg, gu, h, go, *adapters, flags.reshape(total_rows, lanes), index.reshape(shape))
+    f32 = jnp.float32
+    return pl.pallas_call(
+        functools.partial(fused_kernel, members, block_rows),
+        out_shape=jax.ShapeDtypeStruct(shape, f32),
+        in_specs=[pl.BlockSpec(memory_space=pltpu.SMEM)]
+        + [pl.BlockSpec(memory_space=pltpu.HBM)] * len(arrays),
+        out_specs=vmem,
+        scratch_shapes=[pltpu.VMEM(array.shape, array.dtype) for array in arrays]
+        + [
+            pltpu.VMEM((6, two, outer, rows, lanes), f32),
+            pltpu.VMEM((6, outer, rows, lanes), f32),
+            pltpu.VMEM((6, outer - 1, rows, lanes), f32),
+            pltpu.VMEM((6, two, outer, rows, lanes), jnp.bfloat16),
+            pltpu.VMEM((total_rows, lanes), f32),
+            pltpu.VMEM((shape[1], chunk, lanes), f32),
+            pltpu.VMEM(shape, f32),
+            pltpu.VMEM((everyone - 1,) + shape[1:], f32),
+            dma((len(arrays),)),
+            dma((6,)), dma((6,)),
+            dma((6, outer - 1)), dma((6, outer - 1)),
+            dma((6, outer - 1)), dma((6, outer - 1)),
+            dma((6,)), dma((6,)),
+        ]
+        + [dma((everyone - 1,))] * 4,
+        compiler_params=pltpu.CompilerParams(
+            collective_id=0, has_side_effects=True, vmem_limit_bytes=56 * 1024 * 1024
+        ),
+    )(row_of, *arrays)
+
+
 def shards(
     projection_input,
     gate_output_gradient,
@@ -162,23 +445,49 @@
 ):
     x, go = projection_input[0, 0], down_output_gradient[0, 0]
     gg, gu, h = gate_output_gradient[0, 0], up_output_gradient[0, 0], hidden[0, 0]
+    coord_count, members = lax.axis_size("coord"), lax.axis_size("ckpt")
+    adapters = [
+        adapter[0]
+        for adapter in (
+            gate_adapter_first,
+            gate_adapter_second,
+            up_adapter_first,
+            up_adapter_second,
+            down_adapter_first,
+            down_adapter_second,
+        )
+    ]
+    local_len = random_sign_flags.shape[0]
+    block_count = coord_count * members
+    scale = ADAPTER_SCALE * float(local_len * block_count) ** (-0.5)
+    lanes = adapters[0].shape[1]
+    if (
+        block_count <= 32
+        and coord_count % 2 == 0
+        and lanes == 128
+        and x.shape[0] % (16 * coord_count) == 0
+        and x.shape[1] % 256 == 0
+        and gg.shape[0] % 256 == 0
+        and sampled_coordinate_index.shape[0] % (128 * block_count) == 0
+    ):
+        sums = fused(
+            x, gg, gu, h, go, adapters, random_sign_flags, sampled_coordinate_index, coord_count, members
+        )
+        return (scale * sums).reshape(1, -1)
     partials = jnp.stack(
         [
-            matrix_product("uj,jx->ux", x, gate_adapter_first[0]),
-            matrix_product("uj,jx->ux", x, up_adapter_first[0]),
-            matrix_product("do,da->oa", h, down_adapter_first[0]),
-            matrix_product("do,da->oa", gg, gate_adapter_second[0]),
-            matrix_product("do,da->oa", gu, up_adapter_second[0]),
-            matrix_product("uj,jx->ux", go, down_adapter_second[0]),
+            matrix_product("uj,jx->ux", x, adapters[0]),
+            matrix_product("uj,jx->ux", x, adapters[2]),
+            matrix_product("do,da->oa", h, adapters[4]),
+            matrix_product("do,da->oa", gg, adapters[1]),
+            matrix_product("do,da->oa", gu, adapters[3]),
+            matrix_product("uj,jx->ux", go, adapters[5]),
         ]
     )
     products = lax.psum(partials, "coord").astype(jnp.bfloat16)
     kept = project(x, gg, gu, h, go, products, random_sign_flags, sampled_coordinate_index)
-    local_len = random_sign_flags.shape[0]
-    block_count = lax.axis_size("coord") * lax.axis_size("ckpt")
-    me = lax.axis_index("coord") * lax.axis_size("ckpt") + lax.axis_index("ckpt")
+    me = lax.axis_index("coord") * members + lax.axis_index("ckpt")
     parity = lax.population_count((sampled_coordinate_index // local_len) & me) & 1
-    scale = ADAPTER_SCALE * float(local_len * block_count) ** (-0.5)
     kept = jnp.where(parity.reshape(kept.shape) != 0, -scale, scale) * kept
     return lax.psum(kept, ("coord", "ckpt")).reshape(1, -1)
 

time: 175 us -> 67 us (0.38)
  blocking collectives: 134 us -> 0 us
  Pallas kernels: 26.3 us -> 63.8 us
  matrix products: 8.71 us -> 0 us
  local copies, waits for them, and re-layouts: 4.77 us -> 0 us
  other arithmetic: 0.07 us -> 2.79 us
    psum x2 -> x0, blocking collectives: 134 us -> none  [the longest x1 76.3 us: shards(): products = lax.psum(partials, 'coord').astype(jnp.bfloat16)]
    pallas_call x1, Pallas kernels: 26.3 us -> 63.8 us  [fused(): pl.pallas_call(functools.partial(fused_kernel, members, block_rows), out_...]
    dot_general x6 -> x0, matrix products: 8.71 us -> none  [matrix_product(): return jnp.einsum(form, left, right, preferred_element_type=jnp.float32)]
    unnamed x26 -> x0, local copies, waits for them, and re-layouts: 4.77 us -> none
where the time goes in v2:
time: 67 us; the launch traced here: 66.6 us
  Pallas kernels  63.8 us (95%)
  other arithmetic  2.79 us (4%)
    pallas_call x1, Pallas kernels, fused(): pl.pallas_call(functools.partial(fused_kernel, members, block_rows), out_...  63.8 us
    select_n x1, other arithmetic, fused(): row_of = index // lanes % total_rows  1.41 us
    mul x1, other arithmetic, shards(): return (scale * sums).reshape(1, -1)  1.38 us

profile of v2, /device:TPU:0, one launch (start us, length us, event | category | flops | bytes accessed | tf_op | source)
XLA Modules:
  0.0 66.6 jit_solution(7456430412707647698)
XLA Ops:
  0.0 1.4 %add_select_fusion.row_ref = s32[8192]{0:T(1024)} fusion(s32[8192]{0:T(1024)} %param.25), kind=kLoop, calls=%fused_computation | loop fusion | flops 212992 | bytes 65536 | tf_op jit(solution)/shard_map/jit(remainder)/select_n | solution.py:397
  1.4 63.8 %shard_map.127 = f32[16,4,128]{2,1,0:T(4,128)} custom-call(s32[8192]{0:T(1024)} %add_select_fusion.row_ref, bf16[384,512]{1,0:T(8,128)(2,1)} %bitcast.21, bf16[1792,384]{1,0:T(8,128)(2,1)} %bitcast.15, bf16[1792,384]{1,0:T(8,128)(2,1)} %bitcast.16, bf16[1792,384]{1,0:T(8,128)(2,1)} %bitcast.17, bf16[384,512]{1,0:T(8,128)(2,1)} %bitcast.22, ...), custom_call_target="tpu_custom_call" | custom-call | tf_op jit(solution)/shard_map/pallas_call | solution.py:402
  65.3 1.4 %broadcast_multiply_fusion = f32[16,4,128]{2,1,0:T(4,128)} fusion(f32[16,4,128]{2,1,0:T(4,128)} %shard_map.127), kind=kLoop, calls=%fused_computation.11 | loop fusion | flops 8192 | bytes 65536 | tf_op jit(solution)/shard_map/mul | solution.py:476

commit v3 on v2

--- a/solution.py
+++ b/solution.py
@@ -166,13 +166,14 @@
     )
 
 def fused_kernel(
-    members, block_rows, row_ref, *refs
+    members, block_rows, *refs
 ):
     hbm, (sums_ref,), scratch = refs[:13], refs[13:14], refs[14:]
     local, scratch = scratch[:13], scratch[13:]
     (
         part_ref, pair_ref, rest_ref, out_ref, z_ref, picked_ref, kept_ref, got_ref,
         load, send1, recv1, send2, recv2, send3, recv3, send4, recv4, send5, recv5, send6, recv6,
+        row_ref, fetched, *slots,
     ) = scratch
     x_ref, gg_ref, gu_ref, h_ref, go_ref, a1, a2, a3, a4, a5, a6, flags_ref, index_ref = local
     count, two, outer, rows, lanes = part_ref.shape
@@ -305,6 +306,8 @@
         sum_products(i)
         if n >= 2:
             finish_products(order[n - 2])
+    loads[12].wait()
+    row_ref[...] = (index_ref[...] // lanes) % z_ref.shape[0]
     loads[11].wait()
     finish_products(order[4])
     gradient(order[0])
@@ -312,6 +315,14 @@
     for i in order[1:]:
         gradient(i)
 
+    def fetch(n, d):
+        return pltpu.make_async_copy(
+            row_ref.at[(flat + d) % members_all], slots[n], fetched.at[n]
+        )
+
+    for n in range(len(slots)):
+        fetch(n, n + 1).start()
+
     filled = 3 * (width + deep) // block_rows
     total_blocks = z_ref.shape[0] // block_rows
 
@@ -328,16 +339,14 @@
 
     lax.fori_loop(0, block_rows // 8, across, 0)
 
-    loads[12].wait()
     tiles, chunk = kept_ref.shape[1:]
     local_len = z_ref.shape[0] * lanes
     here = lax.broadcasted_iota(jnp.int32, (lanes, chunk), 0)
 
-    def pick(j):
+    def pick(j, slot):
         for q in range(tiles):
-            t = j * tiles + q
             for k in range(chunk):
-                picked_ref[q, pl.ds(k, 1), :] = z_ref[pl.ds(row_ref[t * chunk + k], 1), :]
+                picked_ref[q, pl.ds(k, 1), :] = z_ref[pl.ds(slot[q, k], 1), :]
             index = index_ref[pl.ds(j, 1), q, :]
             chosen = jnp.where(here == (index & (lanes - 1)), picked_ref[q].T, 0.0)
             chosen = jnp.sum(chosen, axis=0, keepdims=True)
@@ -358,16 +367,23 @@
             sums_ref.at[flat], sums_ref.at[flat], send6.at[d - 1], recv6.at[d - 1], member(d)
         )
 
-    def pick_and_send(d, carry):
-        pick((flat + d) % members_all)
-
-        @pl.when(d < members_all)
-        def _():
-            scatter(d).start()
+    def pick_and_send(g, carry):
+        for n in range(len(slots)):
+            d = g * len(slots) + n + 1
+            fetch(n, d).wait()
+            pick((flat + d) % members_all, slots[n])
+
+            @pl.when(d + len(slots) <= members_all)
+            def _():
+                fetch(n, d + len(slots)).start()
+
+            @pl.when(d < members_all)
+            def _():
+                scatter(d).start()
 
         return carry
 
-    lax.fori_loop(1, members_all + 1, pick_and_send, 0)
+    lax.fori_loop(0, members_all // len(slots), pick_and_send, 0)
     total = kept_ref[flat]
     for d in range(1, members_all):
         scatter(d).wait_recv()
@@ -394,7 +410,7 @@
     two, rows = 2, seq // coord_count
     outer, everyone = coord_count // two, coord_count * members
     shape = (everyone, index.shape[0] // (everyone * chunk), chunk)
-    row_of = (index // lanes) % total_rows
+    slots = 4
     vmem = pl.BlockSpec(memory_space=pltpu.VMEM)
     dma = pltpu.SemaphoreType.DMA
     arrays = (x, gg, gu, h, go, *adapters, flags.reshape(total_rows, lanes), index.reshape(shape))
@@ -402,8 +418,7 @@
     return pl.pallas_call(
         functools.partial(fused_kernel, members, block_rows),
         out_shape=jax.ShapeDtypeStruct(shape, f32),
-        in_specs=[pl.BlockSpec(memory_space=pltpu.SMEM)]
-        + [pl.BlockSpec(memory_space=pltpu.HBM)] * len(arrays),
+        in_specs=[pl.BlockSpec(memory_space=pltpu.HBM)] * len(arrays),
         out_specs=vmem,
         scratch_shapes=[pltpu.VMEM(array.shape, array.dtype) for array in arrays]
         + [
@@ -421,11 +436,13 @@
             dma((6, outer - 1)), dma((6, outer - 1)),
             dma((6,)), dma((6,)),
         ]
-        + [dma((everyone - 1,))] * 4,
+        + [dma((everyone - 1,))] * 4
+        + [pltpu.VMEM(shape, jnp.int32), dma((slots,))]
+        + [pltpu.SMEM(shape[1:], jnp.int32)] * slots,
         compiler_params=pltpu.CompilerParams(
             collective_id=0, has_side_effects=True, vmem_limit_bytes=56 * 1024 * 1024
         ),
-    )(row_of, *arrays)
+    )(*arrays)
 
 
 def shards(
@@ -463,6 +480,7 @@
     lanes = adapters[0].shape[1]
     if (
         block_count <= 32
+        and block_count % 4 == 0
         and coord_count % 2 == 0
         and lanes == 128
         and x.shape[0] % (16 * coord_count) == 0

time: 67 us -> 62.8 us (0.937)
  Pallas kernels: 63.8 us -> 61.2 us
  other arithmetic: 2.79 us -> 1.38 us
    pallas_call x1, Pallas kernels: 63.8 us -> 61.2 us  [fused(): pl.pallas_call(functools.partial(fused_kernel, members, block_rows), out_...]
    select_n x1 -> x0, other arithmetic: 1.41 us -> none  [fused(): row_of = index // lanes % total_rows]
where the time goes in v3:
time: 62.8 us; the launch traced here: 62.6 us
  Pallas kernels  61.2 us (97%)
  other arithmetic  1.38 us (2%)
    pallas_call x1, Pallas kernels, fused(): pl.pallas_call(functools.partial(fused_kernel, members, block_rows), out_...  61.2 us
    mul x1, other arithmetic, shards(): return (scale * sums).reshape(1, -1)  1.38 us

profile of v3, /device:TPU:0, one launch (start us, length us, event | category | flops | bytes accessed | tf_op | source)
XLA Modules:
  0.0 62.6 jit_solution(5364190089314728667)
XLA Ops:
  0.0 61.2 %shard_map.127 = f32[16,4,128]{2,1,0:T(4,128)} custom-call(bf16[384,512]{1,0:T(8,128)(2,1)} %bitcast.21, bf16[1792,384]{1,0:T(8,128)(2,1)} %bitcast.15, bf16[1792,384]{1,0:T(8,128)(2,1)} %bitcast.16, bf16[1792,384]{1,0:T(8,128)(2,1)} %bitcast.17, bf16[384,512]{1,0:T(8,128)(2,1)} %bitcast.22, bf16[512,128]{1,0:T(8,128)(2,1)} %bitcast.23, ...), custom_call_target="tpu_custom_call" | custom-call | tf_op jit(solution)/shard_map/pallas_call | solution.py:418
  61.2 1.4 %broadcast_multiply_fusion = f32[16,4,128]{2,1,0:T(4,128)} fusion(f32[16,4,128]{2,1,0:T(4,128)} %shard_map.127), kind=kLoop, calls=%fused_computation | loop fusion | flops 8192 | bytes 65536 | tf_op jit(solution)/shard_map/mul | solution.py:494

commit v4 on v3

--- a/solution.py
+++ b/solution.py
@@ -261,8 +261,7 @@
         span = pl.ds(pl.multiple_of(b * block_rows, block_rows), block_rows)
         value = z_ref[span, :]
         value = jnp.where(flags_ref[span, :] != 0, -value, value)
-        value = dot(jnp.concatenate(halves(value), axis=1), lane_table)
-        return span, dot(row_table, jnp.concatenate(halves(value), axis=0))
+        return span, dot(jnp.concatenate(halves(value), axis=1), lane_table)
 
     def gradient(i):
         finish(i).wait_recv()
@@ -281,8 +280,10 @@
 
         def some(n, at):
             done = [transform(at + k) for k in range(n)]
-            for span, value in done:
-                z_ref[span, :] = value
+            value = jnp.concatenate([value for _, value in done], axis=1)
+            value = dot(row_table, jnp.concatenate(halves(value), axis=0))
+            for k, (span, _) in enumerate(done):
+                z_ref[span, :] = value[:, k * lanes : (k + 1) * lanes]
 
         if blocks >= 2:
 

time: 62.8 us -> 60.1 us (0.957)
  Pallas kernels: 61.2 us -> 58.5 us
    pallas_call x1, Pallas kernels: 61.2 us -> 58.5 us  [fused(): pl.pallas_call(functools.partial(fused_kernel, members, block_rows), out_...]
where the time goes in v4:
time: 60.1 us; the launch traced here: 59.9 us
  Pallas kernels  58.5 us (97%)
  other arithmetic  1.38 us (2%)
    pallas_call x1, Pallas kernels, fused(): pl.pallas_call(functools.partial(fused_kernel, members, block_rows), out_...  58.5 us
    mul x1, other arithmetic, shards(): return (scale * sums).reshape(1, -1)  1.38 us

profile of v4, /device:TPU:0, one launch (start us, length us, event | category | flops | bytes accessed | tf_op | source)
XLA Modules:
  0.0 59.9 jit_solution(17086629500698668739)
XLA Ops:
  0.0 58.5 %shard_map.127 = f32[16,4,128]{2,1,0:T(4,128)} custom-call(bf16[384,512]{1,0:T(8,128)(2,1)} %bitcast.21, bf16[1792,384]{1,0:T(8,128)(2,1)} %bitcast.15, bf16[1792,384]{1,0:T(8,128)(2,1)} %bitcast.16, bf16[1792,384]{1,0:T(8,128)(2,1)} %bitcast.17, bf16[384,512]{1,0:T(8,128)(2,1)} %bitcast.22, bf16[512,128]{1,0:T(8,128)(2,1)} %bitcast.23, ...), custom_call_target="tpu_custom_call" | custom-call | tf_op jit(solution)/shard_map/pallas_call | solution.py:419
  58.5 1.4 %broadcast_multiply_fusion = f32[16,4,128]{2,1,0:T(4,128)} fusion(f32[16,4,128]{2,1,0:T(4,128)} %shard_map.127), kind=kLoop, calls=%fused_computation | loop fusion | flops 8192 | bytes 65536 | tf_op jit(solution)/shard_map/mul | solution.py:495
